TPU v7x, 32 devices: a whole 2x2x4 slice. The times are simulated.
32 devices in a mesh: query: 8 (over z, y), store: 4 (over x, core).
Axes of the slice: x: 2, y: 2, z: 4, core: 2. Of those that a mesh axis runs over, the one named last changes fastest.
Arguments:
- in_rows: bfloat16 [8, 16384, 64], P('query', 'store'), may hold values from -6 to 6
- out_rows: bfloat16 [8, 16384, 128], P('query', 'store'), may hold values from -0.625 to 0.625
- row_doc: int32 [8, 16384], P('query', 'store'), may hold values from 0 to 31
- row_pos: int32 [8, 16384], P('query', 'store'), may hold values from 0 to 255
- doc_len: int32 [8, 128], P('query', 'store'), may hold values from 128 to 256
- eig_in: float32 [64], replicated, may hold values from 0.25 to 2
- eig_out: float32 [128], replicated, may hold values from 0.25 to 2
- basis_in: float32 [64, 64], replicated, may hold values from -0.75 to 0.75
- basis_out: float32 [128, 128], replicated, may hold values from -0.5 to 0.5
- train_feats: bfloat16 [8, 768, 8192], P('query', 'store'), may hold values from -0.0625 to 0.0625
Outputs:
- scores: bfloat16 [8, 128, 768], P('query', None, 'store')
Inputs may be any that keep to these rules, and one draw needn't show every extreme that they name: On each device the 4096 rows form 8 blocks of 512 rows in order; the rows of block j belong to documents of group j in the same store column, and row_doc names the document among that destination's 32.
All inputs are finite; a program needn't handle non-finite values.
Results may differ from a plain program's by a relative error of at most 0.0049.
Values may be sent and summed in bfloat16 or wider, within the bound.
A program may use at most 64 MiB of HBM per device.

v0:
```python
import math
import jax
import jax.numpy as jnp
from jax import lax
from jax.sharding import PartitionSpec as P

damping = 0.1
highest = lax.Precision.HIGHEST


def from_behind(x, axis, by):
    devices = lax.axis_size(axis)
    return lax.ppermute(x, axis, [(i, (i + by) % devices) for i in range(devices)])


def precondition(gradients, scaling, basis_in, basis_out):
    in_width = basis_in.shape[0]
    out_width = basis_out.shape[0]
    doc_count = gradients.shape[1] // in_width
    rotated = jnp.dot(basis_out.T, gradients, precision=highest)
    turned = jnp.dot(rotated.reshape(out_width * doc_count, in_width), basis_in, precision=highest)
    turned = turned.reshape(out_width, doc_count, in_width) * scaling[:, None, :]
    restored = jnp.dot(
        basis_out, turned.reshape(out_width, doc_count * in_width), precision=highest
    )
    final_map = jnp.dot(
        restored.reshape(out_width * doc_count, in_width), basis_in.T, precision=highest
    )
    final_map = final_map.reshape(out_width, doc_count, in_width)
    return (
        jnp.transpose(final_map, (1, 0, 2))
        .reshape(doc_count, out_width * in_width)
        .astype(jnp.bfloat16)
    )


def record(score_table, query_block, anchor, train_slab):
    partial_scores = lax.dot_general(
        query_block, train_slab, (((1,), (1,)), ((), ())), preferred_element_type=jnp.float32
    )
    return lax.dynamic_update_slice_in_dim(
        score_table, partial_scores.astype(jnp.bfloat16), anchor * query_block.shape[0], 0
    )


def on_device(
    in_rows, out_rows, row_doc, row_pos, doc_len, eig_in, eig_out, basis_in, basis_out, train_feats
):
    doc_count = doc_len.shape[1]
    in_width = in_rows.shape[2]
    packed_keys = row_doc * 65536 + row_pos
    inputs_side, grads_side, keys_side = (
        lax.all_to_all(in_rows, "query", split_axis=1, concat_axis=1, tiled=True),
        lax.all_to_all(out_rows, "query", split_axis=1, concat_axis=1, tiled=True),
        lax.all_to_all(packed_keys, "query", split_axis=1, concat_axis=1, tiled=True),
    )
    inputs_side = inputs_side[0]
    grads_side = grads_side[0]
    keys_side = keys_side[0]
    doc_of_row = keys_side // 65536
    pos_of_row = keys_side % 65536
    live_mask = (doc_of_row[:, None] == jnp.arange(doc_count, dtype=jnp.int32)[None, :]) & (
        pos_of_row[:, None] < doc_len[0][None, :]
    )
    weights = live_mask.astype(jnp.bfloat16)
    row_count = inputs_side.shape[0]
    row_span = math.gcd(row_count, 1024)

    def accumulate(turn_index, running):
        row_start = turn_index * row_span
        x_part = lax.dynamic_slice_in_dim(inputs_side, row_start, row_span, 0)
        g_part = lax.dynamic_slice_in_dim(grads_side, row_start, row_span, 0)
        w_part = lax.dynamic_slice_in_dim(weights, row_start, row_span, 0)
        spread = (w_part[:, :, None] * x_part[:, None, :]).reshape(row_span, doc_count * in_width)
        return running + lax.dot_general(
            g_part, spread, (((0,), (0,)), ((), ())), preferred_element_type=jnp.float32
        )

    gradients = jnp.zeros((grads_side.shape[1], doc_count * in_width), jnp.float32)
    gradients = lax.fori_loop(0, row_count // row_span, accumulate, gradients)
    scaling = 1.0 / (eig_out[:, None] * eig_in[None, :] + damping)
    query_block = precondition(gradients, scaling, basis_in, basis_out)
    train_slab = train_feats[0]
    store_count = lax.axis_size("store")
    own_index = lax.axis_index("store")
    score_table = jnp.zeros((store_count * doc_count, train_slab.shape[0]), jnp.bfloat16)

    def travel(carry, visit_index):
        moving, table_now = carry
        table_now = record(table_now, moving, (own_index - visit_index) % store_count, train_slab)
        moving = from_behind(moving, "store", 1)
        return ((moving, table_now), None)

    (moving, score_table), _ = lax.scan(
        travel, (query_block, score_table), jnp.arange(store_count - 1, dtype=jnp.int32)
    )
    score_table = record(
        score_table, moving, (own_index - (store_count - 1)) % store_count, train_slab
    )
    return score_table[None]


def solution(mesh):
    placed = (
        P("query", "store", None),
        P("query", "store", None),
        P("query", "store"),
        P("query", "store"),
        P("query", "store"),
        P(),
        P(),
        P(),
        P(),
        P("query", "store", None),
    )
    return jax.shard_map(
        on_device, mesh=mesh, in_specs=placed, out_specs=P("query", None, "store"), check_vma=False
    )
```

profile of v0, /device:TPU:0, one launch (start us, length us, event | category | flops | bytes accessed | tf_op | source)
XLA Modules:
  0.0 183.5 jit_solution(18066739965186172153)
XLA Ops:
  1.4 7.3 %all-to-all-start.1 = ((s32[1,8,512]{2,0,1:T(1,128)}), s32[1,8,512]{2,0,1:T(1,128)S(1)}, u32[]{:S(2)}, u32[]{:S(2)}) async-start(s32[1,8,512]{2,0,1:T(1,128)} %bitcast.1), calls=%async_computation.1 | async-start | bytes 32768 | tf_op jit(solution)/shard_map/all_to_all | solution.py:55
  8.7 4.9 %copy.27 = bf16[1,4096,64]{2,0,1:T(2,128)(2,1)S(1)} copy(bf16[1,4096,64]{1,2,0:T(8,128)(2,1)} %param.14) | data formatting | bytes 1048576 | tf_op args[0]
  14.1 22.3 %reduce.1 = bf16[4096,64]{1,0:T(8,128)(2,1)S(1)} reduce(bf16[4096,1,64]{2,1,0:T(2,128)(2,1)S(1)} %bitcast.60, bf16[]{:T(256)} %broadcast.96), dimensions={1}, to_apply=%bitcast.31.reduce_sub_computation | reduce | bytes 1048578
  37.9 6.0 %all-to-all-start.2 = ((bf16[8,2,16384]{2,1,0:T(2,128)(2,1)}), bf16[8,2,16384]{2,1,0:T(2,128)(2,1)}, u32[]{:S(2)}, u32[]{:S(2)}) async-start(bf16[8,2,16384]{2,1,0:T(2,128)(2,1)} %reshape.110), calls=%async_computation.2 | async-start | bytes 1048576 | tf_op jit(solution)/shard_map/all_to_all | solution.py:53
  43.9 3.2 %copy.39 = bf16[1,4096,128]{2,0,1:T(2,128)(2,1)S(1)} copy(bf16[1,4096,128]{2,1,0:T(8,128)(2,1)} %param.15) | data formatting | bytes 2097152 | tf_op args[1]
  47.1 22.3 %reduce = bf16[4096,128]{1,0:T(8,128)(2,1)S(1)} reduce(bf16[4096,1,128]{2,1,0:T(2,128)(2,1)S(1)} %bitcast.62, bf16[]{:T(256)} %broadcast.96), dimensions={1}, to_apply=%bitcast.45.reduce_sub_computation | reduce | bytes 2097154
  70.6 6.0 %all-to-all-start = ((bf16[8,2,32768]{2,1,0:T(2,128)(2,1)}), bf16[8,2,32768]{2,1,0:T(2,128)(2,1)}, u32[]{:S(2)}, u32[]{:S(2)}) async-start(bf16[8,2,32768]{2,1,0:T(2,128)(2,1)} %reshape.108), calls=%async_computation | async-start | bytes 2097152 | tf_op jit(solution)/shard_map/all_to_all | solution.py:54
  76.9 4.1 %reshape.111 = bf16[4096,1,64]{2,1,0:T(2,128)(2,1)S(1)} reshape(bf16[8,2,16384]{2,1,0:T(2,128)(2,1)} %all-to-all-done.2) | data formatting | bytes 1048576
  81.0 3.6 %copy.28 = bf16[1,4096,64]{1,2,0:T(8,128)(2,1)} copy(bf16[1,4096,64]{2,0,1:T(2,128)(2,1)S(1)} %bitcast.59) | data formatting | bytes 1048576 | tf_op jit(solution)/shard_map/all_to_all | solution.py:53
  84.7 16.9 %all-to-all-done = bf16[8,2,32768]{2,1,0:T(2,128)(2,1)} async-done(((bf16[8,2,32768]{2,1,0:T(2,128)(2,1)}), bf16[8,2,32768]{2,1,0:T(2,128)(2,1)}, u32[]{:S(2)}, u32[]{:S(2)}) %all-to-all-start) | async-done | bytes 1048608 | tf_op jit(solution)/shard_map/all_to_all | solution.py:54
  101.5 4.3 %reshape.109 = bf16[4096,1,128]{2,1,0:T(2,128)(2,1)S(1)} reshape(bf16[8,2,32768]{2,1,0:T(2,128)(2,1)} %all-to-all-done) | data formatting | bytes 2097152
  107.0 28.7 %while.29 = (s32[]{:T(128)}, f32[128,2048]{1,0:T(8,128)S(1)}, bf16[4096,128]{1,0:T(8,128)(2,1)}, bf16[4096,32]{0,1:T(8,128)(2,1)S(1)}, bf16[4096,64]{0,1:T(8,128...) while((s32[]{:T(128)}, f32[128,2048]{1,0:T(8,128)S(1)}, bf16[4096,128]{1,0:T(8,128)(2,1)}, ...), condition=%wide.region_1.2_spmd.clone, body=%wide.region_0.1_spmd.clone.sunk | while | flops 539492352 | bytes 11337897 | solution.py:80
  107.9 2.2 %broadcast_multiply_fusion.2 = bf16[1024,32,64]{0,2,1:T(8,128)(2,1)} fusion(bf16[1024,64]{0,1:T(8,128)(2,1)S(1)} %constant_dynamic-slice_fusion.4, bf16[1024,32]{0,1:T(8,128)(2,1)S(1)} %constant_dynamic-slice_fusion.5), kind=kLoop, calls=%fused_computation.3.clone.1 | loop fusion | flops 2097152 | bytes 4390912 | tf_op jit(solution)/shard_map/while/body/eval_jaxpr/mul | solution.py:74
  110.1 4.0 %convolution_add_fusion.2 = f32[128,2048]{1,0:T(8,128)S(1)} fusion(bf16[1024,2048]{0,1:T(8,128)(2,1)} %bitcast.56, f32[128,2048]{1,0:T(8,128)S(1)} %get-tuple-element.306, pred[]{:T(512)S(6)} %compare.16, bf16[4096,128]{1,0:T(8,128)(2,1)} %get-tuple-element.316, s32[]{:T(128)S(6)} %select_n.65), kind=kOutput, calls=%fused_computation.2.clone.1 | convolution fusion | flops 537395200 | bytes 6553605 | tf_op jit(solution)/shard_map/while/body/eval_jaxpr/dot_general | solution.py:75
  115.1 2.2 %broadcast_multiply_fusion.2 = bf16[1024,32,64]{0,2,1:T(8,128)(2,1)} fusion(bf16[1024,64]{0,1:T(8,128)(2,1)S(1)} %constant_dynamic-slice_fusion.4, bf16[1024,32]{0,1:T(8,128)(2,1)S(1)} %constant_dynamic-slice_fusion.5), kind=kLoop, calls=%fused_computation.3.clone.1 | loop fusion | flops 2097152 | bytes 4390912 | tf_op jit(solution)/shard_map/while/body/eval_jaxpr/mul | solution.py:74
  117.3 4.0 %convolution_add_fusion.2 = f32[128,2048]{1,0:T(8,128)S(1)} fusion(bf16[1024,2048]{0,1:T(8,128)(2,1)} %bitcast.56, f32[128,2048]{1,0:T(8,128)S(1)} %get-tuple-element.306, pred[]{:T(512)S(6)} %compare.16, bf16[4096,128]{1,0:T(8,128)(2,1)} %get-tuple-element.316, s32[]{:T(128)S(6)} %select_n.65), kind=kOutput, calls=%fused_computation.2.clone.1 | convolution fusion | flops 537395200 | bytes 6553605 | tf_op jit(solution)/shard_map/while/body/eval_jaxpr/dot_general | solution.py:75
  124.5 4.0 %convolution_add_fusion.2 = f32[128,2048]{1,0:T(8,128)S(1)} fusion(bf16[1024,2048]{0,1:T(8,128)(2,1)} %bitcast.56, f32[128,2048]{1,0:T(8,128)S(1)} %get-tuple-element.306, pred[]{:T(512)S(6)} %compare.16, bf16[4096,128]{1,0:T(8,128)(2,1)} %get-tuple-element.316, s32[]{:T(128)S(6)} %select_n.65), kind=kOutput, calls=%fused_computation.2.clone.1 | convolution fusion | flops 537395200 | bytes 6553605 | tf_op jit(solution)/shard_map/while/body/eval_jaxpr/dot_general | solution.py:75
  131.7 4.0 %convolution_add_fusion.2 = f32[128,2048]{1,0:T(8,128)S(1)} fusion(bf16[1024,2048]{0,1:T(8,128)(2,1)} %bitcast.56, f32[128,2048]{1,0:T(8,128)S(1)} %get-tuple-element.306, pred[]{:T(512)S(6)} %compare.16, bf16[4096,128]{1,0:T(8,128)(2,1)} %get-tuple-element.316, s32[]{:T(128)S(6)} %select_n.65), kind=kOutput, calls=%fused_computation.2.clone.1 | convolution fusion | flops 537395200 | bytes 6553605 | tf_op jit(solution)/shard_map/while/body/eval_jaxpr/dot_general | solution.py:75
  141.5 2.4 %copy.30 = bf16[32,128,64]{2,1,0:T(8,128)(2,1)} copy(bf16[32,128,64]{1,2,0:T(8,128)(2,1)} %fusion.3) | data formatting | bytes 1048576 | tf_op jit(solution)/shard_map/convert_element_type | solution.py:33
  143.9 2.7 %convert_element_type.24 = bf16[32,8192]{1,0:T(8,128)(2,1)} reshape(bf16[32,128,64]{2,1,0:T(8,128)(2,1)} %copy.30) | data formatting | bytes 1048576 | tf_op jit(solution)/shard_map/convert_element_type | solution.py:33
  146.6 32.4 %while.28 = (s32[]{:T(128)}, bf16[32,8192]{1,0:T(8,128)(2,1)}, bf16[128,192]{1,0:T(8,128)(2,1)S(1)}, bf16[192,8192]{1,0:T(8,128)(2,1)S(1)}, s32[3]{0:T(128)S(1)}...) while((s32[]{:T(128)}, bf16[32,8192]{1,0:T(8,128)(2,1)}, ...), condition=%wide.region_3.4_spmd, body=%wide.region_2.3_spmd.sunk | while | flops 100669456 | bytes 6832468 | solution.py:94
  151.8 5.6 %collective-permute-done = bf16[32,8192]{1,0:T(8,128)(2,1)} collective-permute-done((bf16[32,8192]{1,0:T(8,128)(2,1)}, bf16[32,8192]{1,0:T(8,128)(2,1)}, u32[]{:S(2)}, u32[]{:S(2)}) %collective-permute-start) | collective-permute-done | bytes 524320 | tf_op jit(solution)/shard_map/while/body/eval_jaxpr/ppermute | solution.py:13
  162.6 5.6 %collective-permute-done = bf16[32,8192]{1,0:T(8,128)(2,1)} collective-permute-done((bf16[32,8192]{1,0:T(8,128)(2,1)}, bf16[32,8192]{1,0:T(8,128)(2,1)}, u32[]{:S(2)}, u32[]{:S(2)}) %collective-permute-start) | collective-permute-done | bytes 524320 | tf_op jit(solution)/shard_map/while/body/eval_jaxpr/ppermute | solution.py:13
  173.4 5.6 %collective-permute-done = bf16[32,8192]{1,0:T(8,128)(2,1)} collective-permute-done((bf16[32,8192]{1,0:T(8,128)(2,1)}, bf16[32,8192]{1,0:T(8,128)(2,1)}, u32[]{:S(2)}, u32[]{:S(2)}) %collective-permute-start) | collective-permute-done | bytes 524320 | tf_op jit(solution)/shard_map/while/body/eval_jaxpr/ppermute | solution.py:13
  (55 shorter events, 38.1 us)
Async XLA Ops:
  0.0 135.7 %copy-start = (f32[128,128]{1,0:T(8,128)S(1)}, f32[128,128]{1,0:T(8,128)}, u32[]{:S(2)}) copy-start(f32[128,128]{1,0:T(8,128)} %param.22) | copy-start | bytes 196612
  1.4 36.5 %all-to-all-start.1 = ((s32[1,8,512]{2,0,1:T(1,128)}), s32[1,8,512]{2,0,1:T(1,128)S(1)}, u32[]{:S(2)}, u32[]{:S(2)}) async-start(s32[1,8,512]{2,0,1:T(1,128)} %bitcast.1), calls=%async_computation.1 | async-start | bytes 32768 | tf_op jit(solution)/shard_map/all_to_all | solution.py:55
  37.9 32.6 %all-to-all-start.2 = ((bf16[8,2,16384]{2,1,0:T(2,128)(2,1)}), bf16[8,2,16384]{2,1,0:T(2,128)(2,1)}, u32[]{:S(2)}, u32[]{:S(2)}) async-start(bf16[8,2,16384]{2,1,0:T(2,128)(2,1)} %reshape.110), calls=%async_computation.2 | async-start | bytes 1048576 | tf_op jit(solution)/shard_map/all_to_all | solution.py:53
  47.1 29.5 %copy-start.3 = (f32[64]{0:T(128)S(1)}, f32[64]{0:T(128)}, u32[]{:S(2)}) copy-start(f32[64]{0:T(128)} %param.19) | copy-start | bytes 772
  47.1 29.5 %copy-start.4 = (f32[128]{0:T(128)S(1)}, f32[128]{0:T(128)}, u32[]{:S(2)}) copy-start(f32[128]{0:T(128)} %param.20) | copy-start | bytes 1540
  47.1 29.6 %copy-start.5 = (s32[1,32]{1,0:T(1,128)S(1)}, s32[1,32]{1,0:T(1,128)}, u32[]{:S(2)}) copy-start(s32[1,32]{1,0:T(1,128)} %param.18) | copy-start | bytes 388
  70.6 31.0 %all-to-all-start = ((bf16[8,2,32768]{2,1,0:T(2,128)(2,1)}), bf16[8,2,32768]{2,1,0:T(2,128)(2,1)}, u32[]{:S(2)}, u32[]{:S(2)}) async-start(bf16[8,2,32768]{2,1,0:T(2,128)(2,1)} %reshape.108), calls=%async_computation | async-start | bytes 2097152 | tf_op jit(solution)/shard_map/all_to_all | solution.py:54
  107.0 30.5 %copy-start.2 = (f32[64,64]{1,0:T(8,128)S(1)}, f32[64,64]{1,0:T(8,128)}, u32[]{:S(2)}) copy-start(f32[64,64]{1,0:T(8,128)} %param.21) | copy-start | bytes 49156
  138.6 8.0 %copy-start.1 = (bf16[1,192,8192]{2,1,0:T(8,128)(2,1)S(1)}, bf16[1,192,8192]{2,1,0:T(8,128)(2,1)}, u32[]{:S(2)}) copy-start(bf16[1,192,8192]{2,1,0:T(8,128)(2,1)} %param.23) | copy-start | bytes 9437188
  148.5 8.9 %collective-permute-start = (bf16[32,8192]{1,0:T(8,128)(2,1)}, bf16[32,8192]{1,0:T(8,128)(2,1)}, u32[]{:S(2)}, u32[]{:S(2)}) collective-permute-start(bf16[32,8192]{1,0:T(8,128)(2,1)} %copy.51), channel_id=1, source_target_pairs={{0,1},{1,2},{2,3},{3,0},{4,5},{5,6},{6,7},{7,4},{8,9},{9,10},{10,1... | collective-permute-start | bytes 1572872 | tf_op jit(solution)/shard_map/while/body/eval_jaxpr/ppermute | solution.py:13
  159.3 8.9 %collective-permute-start = (bf16[32,8192]{1,0:T(8,128)(2,1)}, bf16[32,8192]{1,0:T(8,128)(2,1)}, u32[]{:S(2)}, u32[]{:S(2)}) collective-permute-start(bf16[32,8192]{1,0:T(8,128)(2,1)} %copy.51), channel_id=1, source_target_pairs={{0,1},{1,2},{2,3},{3,0},{4,5},{5,6},{6,7},{7,4},{8,9},{9,10},{10,1... | collective-permute-start | bytes 1572872 | tf_op jit(solution)/shard_map/while/body/eval_jaxpr/ppermute | solution.py:13
  170.1 8.9 %collective-permute-start = (bf16[32,8192]{1,0:T(8,128)(2,1)}, bf16[32,8192]{1,0:T(8,128)(2,1)}, u32[]{:S(2)}, u32[]{:S(2)}) collective-permute-start(bf16[32,8192]{1,0:T(8,128)(2,1)} %copy.51), channel_id=1, source_target_pairs={{0,1},{1,2},{2,3},{3,0},{4,5},{5,6},{6,7},{7,4},{8,9},{9,10},{10,1... | collective-permute-start | bytes 1572872 | tf_op jit(solution)/shard_map/while/body/eval_jaxpr/ppermute | solution.py:13
where the time goes:
time: 185 us; the launch traced here: 184 us
  other arithmetic  55.2 us (30%)
  local copies, waits for them, and re-layouts  43 us (23%)
  waiting for transfers between devices  33.7 us (18%)
  matrix products  30.1 us (16%)
  starting transfers between devices  19.3 us (10%)
  loops' own time  1.96 us (1%)
    unnamed x3, other arithmetic  44.6 us
    unnamed x20, local copies, waits for them, and re-layouts  20.8 us
    all_to_all x1, waiting for transfers between devices, on_device(): lax.all_to_all(out_rows, 'query', split_axis=1, concat_axis=1, tiled=True)  16.9 us
    ppermute x3, waiting for transfers between devices, from_behind(): lax.ppermute(x, axis, [(i, (i + by) % devices) for i in range(devices)])  16.9 us
    dot_general x4, matrix products, accumulate(): lax.dot_general(g_part, spread, (((0,), (0,)), ((), ())), preferred_eleme...  15.9 us
    mul x4, other arithmetic, accumulate(): w_part[:, :, None] * x_part[:, None, :]  8.93 us
    dot_general x4, matrix products, record(): lax.dot_general(query_block, train_slab, (((1,), (1,)), ((), ())), prefer...  8.42 us
    all_to_all x1, starting transfers between devices, on_device(): lax.all_to_all(packed_keys, 'query', split_axis=1, concat_axis=1, tiled=T...  7.31 us
  transfers between devices with their start and end apart: 6, of which 4 were waited for; matrix products, arithmetic and copies ran while one was open for 39% of the time, Pallas kernels for 0%

commit v1 on v0

--- a/solution.py
+++ b/solution.py
@@ -50,7 +50,12 @@
     in_width = in_rows.shape[2]
     packed_keys = row_doc * 65536 + row_pos
     inputs_side, grads_side, keys_side = (
-        lax.all_to_all(in_rows, "query", split_axis=1, concat_axis=1, tiled=True),
+        jnp.concatenate(
+            lax.all_to_all(
+                jnp.stack(jnp.split(in_rows, lax.axis_size("query"), axis=1)), "query", 0, 0
+            ),
+            axis=1,
+        ),
         lax.all_to_all(out_rows, "query", split_axis=1, concat_axis=1, tiled=True),
         lax.all_to_all(packed_keys, "query", split_axis=1, concat_axis=1, tiled=True),
     )

time: 185 us -> 168 us (0.908)
  other arithmetic: 55.2 us -> 33 us
  waiting for transfers between devices: 33.7 us -> 39.1 us
    unnamed x3 -> x2, other arithmetic: 44.6 us -> 22.4 us
    all_to_all x1, waiting for transfers between devices: 16.9 us -> 22.7 us  [on_device(): lax.all_to_all(out_rows, 'query', split_axis=1, concat_axis=1, tiled=True)]
    all_to_all x1 -> x0, local copies, waits for them, and re-layouts: 3.63 us -> none  [on_device(): lax.all_to_all(in_rows, 'query', split_axis=1, concat_axis=1, tiled=True)]
    unnamed x20 -> x25, local copies, waits for them, and re-layouts: 20.8 us -> 22.4 us
    another operation x3 -> x4, local copies, waits for them, and re-layouts: 5.6 us -> 7.08 us
  transfers between devices with their start and end apart: 6 -> 6, of which waited for: 4 -> 4; matrix products, arithmetic and copies ran while one was open for 39% -> 30% of each run, Pallas kernels for 0% -> 0%
where the time goes in v1:
time: 168 us; the launch traced here: 167 us
  local copies, waits for them, and re-layouts  42.6 us (25%)
  waiting for transfers between devices  39.1 us (23%)
  other arithmetic  33 us (20%)
  matrix products  30.2 us (18%)
  starting transfers between devices  19.3 us (11%)
  loops' own time  2.26 us (1%)
    all_to_all x1, waiting for transfers between devices, on_device(): lax.all_to_all(out_rows, 'query', split_axis=1, concat_axis=1, tiled=True)  22.7 us
    unnamed x2, other arithmetic  22.4 us
    unnamed x25, local copies, waits for them, and re-layouts  22.4 us
    ppermute x3, waiting for transfers between devices, from_behind(): lax.ppermute(x, axis, [(i, (i + by) % devices) for i in range(devices)])  16.4 us
    dot_general x4, matrix products, accumulate(): lax.dot_general(g_part, spread, (((0,), (0,)), ((), ())), preferred_eleme...  16 us
    mul x4, other arithmetic, accumulate(): w_part[:, :, None] * x_part[:, None, :]  8.92 us
    dot_general x4, matrix products, record(): lax.dot_general(query_block, train_slab, (((1,), (1,)), ((), ())), prefer...  8.42 us
    all_to_all x1, starting transfers between devices, on_device(): lax.all_to_all(packed_keys, 'query', split_axis=1, concat_axis=1, tiled=T...  7.31 us
  transfers between devices with their start and end apart: 6, of which 4 were waited for; matrix products, arithmetic and copies ran while one was open for 30% of the time, Pallas kernels for 0%

profile of v1, /device:TPU:0, one launch (start us, length us, event | category | flops | bytes accessed | tf_op | source)
XLA Modules:
  0.0 166.7 jit_solution(5619117374517007296)
XLA Ops:
  1.4 7.3 %all-to-all-start.1 = ((s32[1,8,512]{2,0,1:T(1,128)}), s32[1,8,512]{2,0,1:T(1,128)S(1)}, u32[]{:S(2)}, u32[]{:S(2)}) async-start(s32[1,8,512]{2,0,1:T(1,128)} %bitcast.1), calls=%async_computation.1 | async-start | bytes 32768 | tf_op jit(solution)/shard_map/all_to_all | solution.py:60
  20.4 6.0 %all-to-all-start.2 = ((bf16[8,1,512,64]{2,3,1,0:T(8,128)(2,1)}), bf16[8,1,512,64]{2,3,1,0:T(8,128)(2,1)}, u32[]{:S(2)}, u32[]{:S(2)}) async-start(bf16[8,1,512,64]{2,3,1,0:T(8,128)(2,1)} %bitcast_dynamic-update-slice_fusion), calls=%async_computation.2 | async-start | bytes 1048576 | tf_op jit(solution)/shard_map/all_to_all | solution.py:54
  26.4 3.2 %copy.40 = bf16[1,4096,128]{2,0,1:T(2,128)(2,1)S(1)} copy(bf16[1,4096,128]{2,1,0:T(8,128)(2,1)} %param.15) | data formatting | bytes 2097152 | tf_op args[1]
  30.1 22.4 %reduce = bf16[4096,128]{1,0:T(8,128)(2,1)S(1)} reduce(bf16[4096,1,128]{2,1,0:T(2,128)(2,1)S(1)} %bitcast.79, bf16[]{:T(256)} %broadcast.96), dimensions={1}, to_apply=%bitcast.64.reduce_sub_computation | reduce | bytes 2097154
  53.7 6.0 %all-to-all-start = ((bf16[8,2,32768]{2,1,0:T(2,128)(2,1)}), bf16[8,2,32768]{2,1,0:T(2,128)(2,1)}, u32[]{:S(2)}, u32[]{:S(2)}) async-start(bf16[8,2,32768]{2,1,0:T(2,128)(2,1)} %reshape.108), calls=%async_computation | async-start | bytes 2097152 | tf_op jit(solution)/shard_map/all_to_all | solution.py:59
  61.9 22.7 %all-to-all-done = bf16[8,2,32768]{2,1,0:T(2,128)(2,1)} async-done(((bf16[8,2,32768]{2,1,0:T(2,128)(2,1)}), bf16[8,2,32768]{2,1,0:T(2,128)(2,1)}, u32[]{:S(2)}, u32[]{:S(2)}) %all-to-all-start) | async-done | bytes 1048608 | tf_op jit(solution)/shard_map/all_to_all | solution.py:59
  84.6 4.3 %reshape.109 = bf16[4096,1,128]{2,1,0:T(2,128)(2,1)S(1)} reshape(bf16[8,2,32768]{2,1,0:T(2,128)(2,1)} %all-to-all-done) | data formatting | bytes 2097152
  90.0 28.8 %while.29 = (s32[]{:T(128)}, f32[128,2048]{1,0:T(8,128)S(1)}, bf16[4096,128]{1,0:T(8,128)(2,1)}, bf16[4096,32]{0,1:T(8,128)(2,1)S(1)}, bf16[4096,64]{0,1:T(8,128...) while((s32[]{:T(128)}, f32[128,2048]{1,0:T(8,128)S(1)}, bf16[4096,128]{1,0:T(8,128)(2,1)}, ...), condition=%wide.region_1.2_spmd.clone, body=%wide.region_0.1_spmd.clone.sunk | while | flops 539492352 | bytes 11337897 | solution.py:85
  91.0 2.2 %broadcast_multiply_fusion.2 = bf16[1024,32,64]{0,2,1:T(8,128)(2,1)} fusion(bf16[1024,64]{0,1:T(8,128)(2,1)S(1)} %constant_dynamic-slice_fusion.4, bf16[1024,32]{0,1:T(8,128)(2,1)S(1)} %constant_dynamic-slice_fusion.5), kind=kLoop, calls=%fused_computation.3.clone.1 | loop fusion | flops 2097152 | bytes 4390912 | tf_op jit(solution)/shard_map/while/body/eval_jaxpr/mul | solution.py:79
  93.2 4.0 %convolution_add_fusion.2 = f32[128,2048]{1,0:T(8,128)S(1)} fusion(bf16[1024,2048]{0,1:T(8,128)(2,1)} %bitcast.75, f32[128,2048]{1,0:T(8,128)S(1)} %get-tuple-element.301, pred[]{:T(512)S(6)} %compare.16, bf16[4096,128]{1,0:T(8,128)(2,1)} %get-tuple-element.311, s32[]{:T(128)S(6)} %select_n.65), kind=kOutput, calls=%fused_computation.2.clone.1 | convolution fusion | flops 537395200 | bytes 6553605 | tf_op jit(solution)/shard_map/while/body/eval_jaxpr/dot_general | solution.py:80
  98.2 2.2 %broadcast_multiply_fusion.2 = bf16[1024,32,64]{0,2,1:T(8,128)(2,1)} fusion(bf16[1024,64]{0,1:T(8,128)(2,1)S(1)} %constant_dynamic-slice_fusion.4, bf16[1024,32]{0,1:T(8,128)(2,1)S(1)} %constant_dynamic-slice_fusion.5), kind=kLoop, calls=%fused_computation.3.clone.1 | loop fusion | flops 2097152 | bytes 4390912 | tf_op jit(solution)/shard_map/while/body/eval_jaxpr/mul | solution.py:79
  100.4 4.0 %convolution_add_fusion.2 = f32[128,2048]{1,0:T(8,128)S(1)} fusion(bf16[1024,2048]{0,1:T(8,128)(2,1)} %bitcast.75, f32[128,2048]{1,0:T(8,128)S(1)} %get-tuple-element.301, pred[]{:T(512)S(6)} %compare.16, bf16[4096,128]{1,0:T(8,128)(2,1)} %get-tuple-element.311, s32[]{:T(128)S(6)} %select_n.65), kind=kOutput, calls=%fused_computation.2.clone.1 | convolution fusion | flops 537395200 | bytes 6553605 | tf_op jit(solution)/shard_map/while/body/eval_jaxpr/dot_general | solution.py:80
  105.4 2.2 %broadcast_multiply_fusion.2 = bf16[1024,32,64]{0,2,1:T(8,128)(2,1)} fusion(bf16[1024,64]{0,1:T(8,128)(2,1)S(1)} %constant_dynamic-slice_fusion.4, bf16[1024,32]{0,1:T(8,128)(2,1)S(1)} %constant_dynamic-slice_fusion.5), kind=kLoop, calls=%fused_computation.3.clone.1 | loop fusion | flops 2097152 | bytes 4390912 | tf_op jit(solution)/shard_map/while/body/eval_jaxpr/mul | solution.py:79
  107.6 4.0 %convolution_add_fusion.2 = f32[128,2048]{1,0:T(8,128)S(1)} fusion(bf16[1024,2048]{0,1:T(8,128)(2,1)} %bitcast.75, f32[128,2048]{1,0:T(8,128)S(1)} %get-tuple-element.301, pred[]{:T(512)S(6)} %compare.16, bf16[4096,128]{1,0:T(8,128)(2,1)} %get-tuple-element.311, s32[]{:T(128)S(6)} %select_n.65), kind=kOutput, calls=%fused_computation.2.clone.1 | convolution fusion | flops 537395200 | bytes 6553605 | tf_op jit(solution)/shard_map/while/body/eval_jaxpr/dot_general | solution.py:80
  112.6 2.2 %broadcast_multiply_fusion.2 = bf16[1024,32,64]{0,2,1:T(8,128)(2,1)} fusion(bf16[1024,64]{0,1:T(8,128)(2,1)S(1)} %constant_dynamic-slice_fusion.4, bf16[1024,32]{0,1:T(8,128)(2,1)S(1)} %constant_dynamic-slice_fusion.5), kind=kLoop, calls=%fused_computation.3.clone.1 | loop fusion | flops 2097152 | bytes 4390912 | tf_op jit(solution)/shard_map/while/body/eval_jaxpr/mul | solution.py:79
  114.8 4.0 %convolution_add_fusion.2 = f32[128,2048]{1,0:T(8,128)S(1)} fusion(bf16[1024,2048]{0,1:T(8,128)(2,1)} %bitcast.75, f32[128,2048]{1,0:T(8,128)S(1)} %get-tuple-element.301, pred[]{:T(512)S(6)} %compare.16, bf16[4096,128]{1,0:T(8,128)(2,1)} %get-tuple-element.311, s32[]{:T(128)S(6)} %select_n.65), kind=kOutput, calls=%fused_computation.2.clone.1 | convolution fusion | flops 537395200 | bytes 6553605 | tf_op jit(solution)/shard_map/while/body/eval_jaxpr/dot_general | solution.py:80
  124.6 2.4 %copy.29 = bf16[32,128,64]{2,1,0:T(8,128)(2,1)} copy(bf16[32,128,64]{1,2,0:T(8,128)(2,1)} %fusion.3) | data formatting | bytes 1048576 | tf_op jit(solution)/shard_map/convert_element_type | solution.py:33
  127.0 2.7 %convert_element_type.24 = bf16[32,8192]{1,0:T(8,128)(2,1)} reshape(bf16[32,128,64]{2,1,0:T(8,128)(2,1)} %copy.29) | data formatting | bytes 1048576 | tf_op jit(solution)/shard_map/convert_element_type | solution.py:33
  129.7 32.4 %while.28 = (s32[]{:T(128)}, bf16[32,8192]{1,0:T(8,128)(2,1)}, bf16[128,192]{1,0:T(8,128)(2,1)S(1)}, bf16[192,8192]{1,0:T(8,128)(2,1)S(1)}, s32[3]{0:T(128)S(1)}...) while((s32[]{:T(128)}, bf16[32,8192]{1,0:T(8,128)(2,1)}, ...), condition=%wide.region_3.4_spmd, body=%wide.region_2.3_spmd.sunk | while | flops 100669456 | bytes 6832468 | solution.py:99
  133.0 2.1 %fusion.31 = bf16[128,192]{1,0:T(8,128)(2,1)S(1)} fusion(bf16[128,192]{1,0:T(8,128)(2,1)S(1)} %get-tuple-element.332, s32[]{:T(128)S(6)} %select_n.64, bf16[32,8192]{1,0:T(8,128)(2,1)} %copy.59, bf16[192,8192]{1,0:T(8,128)(2,1)S(1)} %get-tuple-element.345), kind=kOutput, calls=%fused_computation.1.clone.1 | convolution fusion | flops 100669440 | bytes 3686404 | tf_op jit(solution)/shard_map/while/body/eval_jaxpr/dot_general | solution.py:38
  135.1 5.5 %collective-permute-done = bf16[32,8192]{1,0:T(8,128)(2,1)} collective-permute-done((bf16[32,8192]{1,0:T(8,128)(2,1)}, bf16[32,8192]{1,0:T(8,128)(2,1)}, u32[]{:S(2)}, u32[]{:S(2)}) %collective-permute-start) | collective-permute-done | bytes 524320 | tf_op jit(solution)/shard_map/while/body/eval_jaxpr/ppermute | solution.py:13
  143.8 2.1 %fusion.31 = bf16[128,192]{1,0:T(8,128)(2,1)S(1)} fusion(bf16[128,192]{1,0:T(8,128)(2,1)S(1)} %get-tuple-element.332, s32[]{:T(128)S(6)} %select_n.64, bf16[32,8192]{1,0:T(8,128)(2,1)} %copy.59, bf16[192,8192]{1,0:T(8,128)(2,1)S(1)} %get-tuple-element.345), kind=kOutput, calls=%fused_computation.1.clone.1 | convolution fusion | flops 100669440 | bytes 3686404 | tf_op jit(solution)/shard_map/while/body/eval_jaxpr/dot_general | solution.py:38
  145.9 5.5 %collective-permute-done = bf16[32,8192]{1,0:T(8,128)(2,1)} collective-permute-done((bf16[32,8192]{1,0:T(8,128)(2,1)}, bf16[32,8192]{1,0:T(8,128)(2,1)}, u32[]{:S(2)}, u32[]{:S(2)}) %collective-permute-start) | collective-permute-done | bytes 524320 | tf_op jit(solution)/shard_map/while/body/eval_jaxpr/ppermute | solution.py:13
  156.7 5.5 %collective-permute-done = bf16[32,8192]{1,0:T(8,128)(2,1)} collective-permute-done((bf16[32,8192]{1,0:T(8,128)(2,1)}, bf16[32,8192]{1,0:T(8,128)(2,1)}, u32[]{:S(2)}, u32[]{:S(2)}) %collective-permute-start) | collective-permute-done | bytes 524320 | tf_op jit(solution)/shard_map/while/body/eval_jaxpr/ppermute | solution.py:13
  (59 shorter events, 41.7 us)
Async XLA Ops:
  0.0 118.8 %copy-start = (f32[128,128]{1,0:T(8,128)S(1)}, f32[128,128]{1,0:T(8,128)}, u32[]{:S(2)}) copy-start(f32[128,128]{1,0:T(8,128)} %param.22) | copy-start | bytes 196612
  1.4 19.0 %all-to-all-start.1 = ((s32[1,8,512]{2,0,1:T(1,128)}), s32[1,8,512]{2,0,1:T(1,128)S(1)}, u32[]{:S(2)}, u32[]{:S(2)}) async-start(s32[1,8,512]{2,0,1:T(1,128)} %bitcast.1), calls=%async_computation.1 | async-start | bytes 32768 | tf_op jit(solution)/shard_map/all_to_all | solution.py:60
  20.4 33.2 %all-to-all-start.2 = ((bf16[8,1,512,64]{2,3,1,0:T(8,128)(2,1)}), bf16[8,1,512,64]{2,3,1,0:T(8,128)(2,1)}, u32[]{:S(2)}, u32[]{:S(2)}) async-start(bf16[8,1,512,64]{2,3,1,0:T(8,128)(2,1)} %bitcast_dynamic-update-slice_fusion), calls=%async_computation.2 | async-start | bytes 1048576 | tf_op jit(solution)/shard_map/all_to_all | solution.py:54
  30.1 29.6 %copy-start.3 = (f32[64]{0:T(128)S(1)}, f32[64]{0:T(128)}, u32[]{:S(2)}) copy-start(f32[64]{0:T(128)} %param.19) | copy-start | bytes 772
  30.1 29.6 %copy-start.4 = (f32[128]{0:T(128)S(1)}, f32[128]{0:T(128)}, u32[]{:S(2)}) copy-start(f32[128]{0:T(128)} %param.20) | copy-start | bytes 1540
  30.1 29.7 %copy-start.5 = (s32[1,32]{1,0:T(1,128)S(1)}, s32[1,32]{1,0:T(1,128)}, u32[]{:S(2)}) copy-start(s32[1,32]{1,0:T(1,128)} %param.18) | copy-start | bytes 388
  53.7 31.0 %all-to-all-start = ((bf16[8,2,32768]{2,1,0:T(2,128)(2,1)}), bf16[8,2,32768]{2,1,0:T(2,128)(2,1)}, u32[]{:S(2)}, u32[]{:S(2)}) async-start(bf16[8,2,32768]{2,1,0:T(2,128)(2,1)} %reshape.108), calls=%async_computation | async-start | bytes 2097152 | tf_op jit(solution)/shard_map/all_to_all | solution.py:59
  90.0 30.6 %copy-start.2 = (f32[64,64]{1,0:T(8,128)S(1)}, f32[64,64]{1,0:T(8,128)}, u32[]{:S(2)}) copy-start(f32[64,64]{1,0:T(8,128)} %param.21) | copy-start | bytes 49156
  121.7 8.0 %copy-start.1 = (bf16[1,192,8192]{2,1,0:T(8,128)(2,1)S(1)}, bf16[1,192,8192]{2,1,0:T(8,128)(2,1)}, u32[]{:S(2)}) copy-start(bf16[1,192,8192]{2,1,0:T(8,128)(2,1)} %param.23) | copy-start | bytes 9437188
  131.6 8.9 %collective-permute-start = (bf16[32,8192]{1,0:T(8,128)(2,1)}, bf16[32,8192]{1,0:T(8,128)(2,1)}, u32[]{:S(2)}, u32[]{:S(2)}) collective-permute-start(bf16[32,8192]{1,0:T(8,128)(2,1)} %copy.59), channel_id=1, source_target_pairs={{0,1},{1,2},{2,3},{3,0},{4,5},{5,6},{6,7},{7,4},{8,9},{9,10},{10,1... | collective-permute-start | bytes 1572872 | tf_op jit(solution)/shard_map/while/body/eval_jaxpr/ppermute | solution.py:13
  142.4 8.9 %collective-permute-start = (bf16[32,8192]{1,0:T(8,128)(2,1)}, bf16[32,8192]{1,0:T(8,128)(2,1)}, u32[]{:S(2)}, u32[]{:S(2)}) collective-permute-start(bf16[32,8192]{1,0:T(8,128)(2,1)} %copy.59), channel_id=1, source_target_pairs={{0,1},{1,2},{2,3},{3,0},{4,5},{5,6},{6,7},{7,4},{8,9},{9,10},{10,1... | collective-permute-start | bytes 1572872 | tf_op jit(solution)/shard_map/while/body/eval_jaxpr/ppermute | solution.py:13
  153.2 8.9 %collective-permute-start = (bf16[32,8192]{1,0:T(8,128)(2,1)}, bf16[32,8192]{1,0:T(8,128)(2,1)}, u32[]{:S(2)}, u32[]{:S(2)}) collective-permute-start(bf16[32,8192]{1,0:T(8,128)(2,1)} %copy.59), channel_id=1, source_target_pairs={{0,1},{1,2},{2,3},{3,0},{4,5},{5,6},{6,7},{7,4},{8,9},{9,10},{10,1... | collective-permute-start | bytes 1572872 | tf_op jit(solution)/shard_map/while/body/eval_jaxpr/ppermute | solution.py:13
